TPU v7x, 32 devices: a whole 2x2x4 slice. The times are simulated.
32 devices in a mesh: groups: 2 (over y), adapter: 16 (over z, x, core).
Axes of the slice: x: 2, y: 2, z: 4, core: 2. Of those that a mesh axis runs over, the one named last changes fastest.
Arguments:
- tokens: bfloat16 [32, 256, 6144], P(('groups', 'adapter')), parts along dimension 0, may hold values from -6 to 6
- base_qkv: bfloat16 [32, 256, 4096], P(('groups', 'adapter')), parts along dimension 0, may hold values from -6 to 6
- cache_keys: bfloat16 [32, 1024, 512], P(('groups', 'adapter')), parts along dimension 0, may hold values from -6 to 6
- cache_values: bfloat16 [32, 1024, 512], P(('groups', 'adapter')), parts along dimension 0, may hold values from -6 to 6
- persona_down: bfloat16 [16, 6144, 64], P('adapter'), may hold values from -0.078125 to 0.078125
- domain_down: bfloat16 [16, 6144, 64], P('adapter'), may hold values from -0.078125 to 0.078125
- persona_up: bfloat16 [16, 4096, 64], P('adapter'), may hold values from -0.29882812 to 0.29882812
- domain_up: bfloat16 [16, 4096, 64], P('adapter'), may hold values from -0.29882812 to 0.29882812
- adapter_ids: int32 [32, 2], P(('groups', 'adapter')), parts along dimension 0, may hold values from 0 to 15
- lengths: int32 [32], P(('groups', 'adapter')), parts along dimension 0, may hold values from 64 to 256, as said below
- offsets: int32 [32], P(('groups', 'adapter')), parts along dimension 0, may hold values from 2 to 1024, as said below
Outputs:
- attended: bfloat16 [32, 256, 3072], P(('groups', 'adapter')), parts along dimension 0
There are 2 independent parts, one for each index of `groups`. A program takes and returns all parts, laid end to end along the dimension named above; an argument that names none is the same for every part. Nothing has to cross between parts.
Inputs may be any that keep to these rules, and one draw needn't show every extreme that they name: `lengths`: each stretch has between 64 and 256 live tokens, the first ones of its slots; some stretch has all 256. `offsets`: each stretch follows between 2 and 1024 cached positions of its prompt, the first ones of its cache; some stretch follows 1024.
All inputs are finite; a program needn't handle non-finite values.
Results may differ from a plain program's by a relative error of at most 0.011.
Values may be sent and summed in bfloat16 or wider, within the bound.
No kernel may reach another device: no remote copies, remote signals or barrier semaphores. Data moves between devices by JAX's collectives and lax.ppermute only.
A program may use at most 128 MiB of HBM per device.

v0:
```python
import functools

import jax
import jax.numpy as jnp
from jax import lax
from jax.experimental import pallas as pl
from jax.experimental.pallas import tpu as pltpu
from jax.sharding import PartitionSpec as P

HEAD_DIM = 128
HEADS = 24
KV_HEADS = 4
GROUP = HEADS // KV_HEADS
STRETCH = 256
CACHE = 1024
ROWS = 8


def attention_kernel(
    offset_ref,
    length_ref,
    low_ref,
    up_q_ref,
    up_k_ref,
    up_v_ref,
    base_q_ref,
    base_k_ref,
    base_v_ref,
    cache_k_ref,
    cache_v_ref,
    out_ref,
    keys,
    values,
    queries,
    bias,
):
    scale = HEAD_DIM ** (-0.5)
    low = low_ref[...]

    @pl.when(pl.program_id(0) == 0)
    def _():
        position = lax.broadcasted_iota(jnp.int32, (STRETCH, CACHE), 1)
        bias[:, :CACHE] = jnp.where(position < offset_ref[0], 0.0, -jnp.inf)
        row = lax.broadcasted_iota(jnp.int32, (STRETCH, STRETCH), 0)
        column = lax.broadcasted_iota(jnp.int32, (STRETCH, STRETCH), 1)
        bias[:, CACHE:] = jnp.where(column <= row, 0.0, -jnp.inf)

    def project(base, up):
        delta = jnp.dot(low, up[...], preferred_element_type=jnp.float32)
        return (base[...].astype(jnp.float32) + delta).astype(jnp.bfloat16)

    keys[:CACHE] = cache_k_ref[...]
    keys[CACHE:] = project(base_k_ref, up_k_ref)
    values[:CACHE] = cache_v_ref[...]
    values[CACHE:] = project(base_v_ref, up_v_ref)
    queries[...] = project(base_q_ref, up_q_ref)
    live = lax.broadcasted_iota(jnp.int32, (STRETCH, HEAD_DIM), 0) < length_ref[0]
    for head in range(GROUP):
        columns = slice(head * HEAD_DIM, (head + 1) * HEAD_DIM)
        scores = lax.dot_general(
            queries[:, columns],
            keys[...],
            (((1,), (1,)), ((), ())),
            preferred_element_type=jnp.float32,
        )
        scores = scores * scale + bias[...]
        row_max = jnp.max(scores, axis=-1, keepdims=True)
        shifted = jnp.exp(scores - row_max)
        row_sum = jnp.sum(shifted, axis=-1, keepdims=True)
        mixed = jnp.dot(
            shifted.astype(jnp.bfloat16), values[...], preferred_element_type=jnp.float32
        )
        mixed = mixed / row_sum
        out_ref[:, columns] = jnp.where(live, mixed, 0.0).astype(out_ref.dtype)


def attention(low, up, base, cache_keys, cache_values, offset, length):
    width = GROUP * HEAD_DIM
    rank2 = low.shape[1]
    key_at = HEADS
    value_at = HEADS + KV_HEADS
    grid_spec = pltpu.PrefetchScalarGridSpec(
        num_scalar_prefetch=2,
        grid=(KV_HEADS,),
        in_specs=[
            pl.BlockSpec((STRETCH, rank2), lambda g, o, n: (0, 0)),
            pl.BlockSpec((rank2, width), lambda g, o, n: (0, g)),
            pl.BlockSpec((rank2, HEAD_DIM), lambda g, o, n: (0, key_at + g)),
            pl.BlockSpec((rank2, HEAD_DIM), lambda g, o, n: (0, value_at + g)),
            pl.BlockSpec((STRETCH, width), lambda g, o, n: (0, g)),
            pl.BlockSpec((STRETCH, HEAD_DIM), lambda g, o, n: (0, key_at + g)),
            pl.BlockSpec((STRETCH, HEAD_DIM), lambda g, o, n: (0, value_at + g)),
            pl.BlockSpec((CACHE, HEAD_DIM), lambda g, o, n: (0, g)),
            pl.BlockSpec((CACHE, HEAD_DIM), lambda g, o, n: (0, g)),
        ],
        out_specs=pl.BlockSpec((STRETCH, width), lambda g, o, n: (0, g)),
        scratch_shapes=[
            pltpu.VMEM((CACHE + STRETCH, HEAD_DIM), jnp.bfloat16),
            pltpu.VMEM((CACHE + STRETCH, HEAD_DIM), jnp.bfloat16),
            pltpu.VMEM((STRETCH, width), jnp.bfloat16),
            pltpu.VMEM((STRETCH, CACHE + STRETCH), jnp.float32),
        ],
    )
    return pl.pallas_call(
        attention_kernel,
        grid_spec=grid_spec,
        out_shape=jax.ShapeDtypeStruct((STRETCH, HEADS * HEAD_DIM), jnp.bfloat16),
        compiler_params=pltpu.CompilerParams(dimension_semantics=("arbitrary",)),
        name="attention",
    )(offset, length, low, up, up, up, base, base, base, cache_keys, cache_values)


def pick_kernel(ids_ref, pool_ref, out_ref, sem):
    copies = [
        pltpu.make_async_copy(pool_ref.at[ids_ref[i]], out_ref.at[i], sem.at[i])
        for i in range(out_ref.shape[0])
    ]
    for copy in copies:
        copy.start()
    for copy in copies:
        copy.wait()


def pick(pool, ids):
    count = ids.shape[0]
    return pl.pallas_call(
        pick_kernel,
        grid_spec=pltpu.PrefetchScalarGridSpec(
            num_scalar_prefetch=1,
            grid=(1,),
            in_specs=[pl.BlockSpec(memory_space=pl.ANY)],
            out_specs=pl.BlockSpec(memory_space=pl.ANY),
            scratch_shapes=[pltpu.SemaphoreType.DMA((count,))],
        ),
        out_shape=jax.ShapeDtypeStruct((count,) + pool.shape[1:], pool.dtype),
        name="pick",
    )(ids, pool)


def fetch_halves(down, up, ids_all):
    group = lax.axis_index("groups")
    index = lax.axis_index("adapter")
    half = index // 8
    rank = down.shape[1]

    def spread(pair):
        mine = jnp.where(group == 0, pair[0], pair[1])
        blocks = mine.reshape(rank // ROWS, ROWS, mine.shape[-1])
        doubled = jnp.concatenate([blocks, blocks], axis=0)
        return lax.all_to_all(doubled, "adapter", 0, 0, tiled=True)

    members = [[g * 16 + h * 8 + k for g in range(2) for k in range(8)] for h in range(2)]
    wanted = lax.dynamic_slice_in_dim(ids_all, half * 8, 8, axis=1)
    wanted = jnp.where(group == 0, wanted[..., 0], wanted[..., 1]).reshape(16)

    def gather(pool):
        picked = pick(pool, wanted)
        got = lax.all_to_all(
            picked, ("groups", "adapter"), 0, 0, tiled=True, axis_index_groups=members
        )
        return got.reshape(2 * rank, pool.shape[-1])

    down_pool = spread(down)
    up_pool = spread(up)
    return gather(down_pool), gather(up_pool)


def fetch_any(down, up, ids_all):
    adapters = ids_all.shape[1]
    group = lax.axis_index("groups")
    rank = down.shape[1]
    parts = adapters // (rank // ROWS)
    wanted = lax.dynamic_index_in_dim(ids_all, group, axis=0, keepdims=False)

    def fetch(pair):
        rows = rank // ROWS
        width = pair.shape[-1] // parts

        def one(factor, ids):
            blocks = factor.reshape(rows, ROWS, parts, width).transpose(0, 2, 1, 3)
            blocks = blocks.reshape(adapters, ROWS, width)
            pool = lax.all_to_all(blocks, "adapter", 0, 0, tiled=True)
            got = lax.all_to_all(jnp.take(pool, ids, axis=0), "adapter", 0, 0, tiled=True)
            got = got.reshape(rows, parts, ROWS, width).transpose(0, 2, 1, 3)
            return got.reshape(rank, parts * width)

        return jnp.concatenate([one(pair[k], wanted[:, k]) for k in range(2)], axis=0)

    return fetch(down), fetch(up)


def body(
    tokens,
    base_qkv,
    cache_keys,
    cache_values,
    persona_down,
    domain_down,
    persona_up,
    domain_up,
    adapter_ids,
    lengths,
    offsets,
    halves,
):
    ids_all = lax.all_gather(adapter_ids, ("groups", "adapter"), axis=0, tiled=True)
    ids_all = ids_all.reshape(2, -1, 2)
    down = (persona_down[0].T, domain_down[0].T)
    up = (persona_up[0].T, domain_up[0].T)
    if halves:
        fetch = fetch_halves
    else:
        fetch = fetch_any
        down = jnp.stack(down)
        up = jnp.stack(up)
    if halves:
        down_mine, up_mine = fetch(_Pair(down), _Pair(up), ids_all)
    else:
        down_mine, up_mine = fetch(down, up, ids_all)
    low = lax.dot_general(
        tokens[0],
        down_mine,
        (((1,), (1,)), ((), ())),
        preferred_element_type=jnp.float32,
    ).astype(jnp.bfloat16)
    out = attention(low, up_mine, base_qkv[0], cache_keys[0], cache_values[0], offsets, lengths)
    return out[None]


class _Pair:
    def __init__(self, items):
        self.items = items
        self.shape = (2,) + items[0].shape

    def __getitem__(self, at):
        return self.items[at]


def solution(mesh):
    both = ("groups", "adapter")
    in_specs = (
        P(both, None, None),
        P(both, None, None),
        P(both, None, None),
        P(both, None, None),
        P("adapter", None, None),
        P("adapter", None, None),
        P("adapter", None, None),
        P("adapter", None, None),
        P(both, None),
        P(both),
        P(both),
    )
    out_specs = P(both, None, None)
    halves = mesh.shape["adapter"] == 16
    return jax.shard_map(
        functools.partial(body, halves=halves),
        mesh=mesh,
        in_specs=in_specs,
        out_specs=out_specs,
        check_vma=False,
    )
```

profile of v0, /device:TPU:0, one launch (start us, length us, event | category | flops | bytes accessed | tf_op | source)
XLA Modules:
  0.0 232.0 jit_solution(10415080629877753795)
XLA Ops:
  0.0 0.0 copy-start
  0.0 1.4 select_bitcast_fusion
  1.4 1.3 pad_maximum_fusion
  2.7 7.4 %all-to-all-start = ((bf16[16,8,6144]{2,1,0:T(8,128)(2,1)}), bf16[16,8,6144]{2,1,0:T(8,128)(2,1)}, u32[]{:S(2)}, u32[]{:S(2)}) async-start(bf16[16,8,6144]{2,1,0:T(8,128)(2,1)} %pad_maximum_fusion), calls=%async_computation | async-start | bytes 3145728 | tf_op jit(solution)/shard_map/all_to_all | solution.py:150
  10.1 1.1 select_bitcast_fusion.1
  11.2 0.0 copy-start.1
  11.2 1.1 pad_maximum_fusion.1
  12.3 29.7 %all-to-all-done.pool_ref = bf16[16,8,6144]{2,1,0:T(8,128)(2,1)} async-done(((bf16[16,8,6144]{2,1,0:T(8,128)(2,1)}), bf16[16,8,6144]{2,1,0:T(8,128)(2,1)}, u32[]{:S(2)}, u32[]{:S(2)}) %all-to-all-start) | async-done | bytes 1572896 | tf_op jit(solution)/shard_map/all_to_all | solution.py:150
  42.0 9.2 %all-to-all-start.2 = ((bf16[16,8,4096]{2,1,0:T(8,128)(2,1)}), bf16[16,8,4096]{2,1,0:T(8,128)(2,1)}, u32[]{:S(2)}, u32[]{:S(2)}) async-start(bf16[16,8,4096]{2,1,0:T(8,128)(2,1)} %pad_maximum_fusion.1), calls=%async_computation.2 | async-start | bytes 2097152 | tf_op jit(solution)/shard_map/all_to_all | solution.py:150
  51.2 0.0 copy-done.1
  51.2 52.8 %all-gather = s32[32,1,2]{2,1,0:T(1,128)S(1)} all-gather(s32[1,1,2]{2,1,0:T(1,128)S(1)} %bitcast.43), channel_id=1, replica_groups=mesh['groups'=2,'adapter'=16] {'groups','adapter'}, dimensions={0}, use_global_device_ids=true | all-gather | bytes 264 | tf_op jit(solution)/shard_map/all_gather | solution.py:206
  104.0 0.1 constant_dynamic-slice_fusion.1
  104.1 0.1 copy.19
  104.2 0.1 copy.20
  104.3 0.6 select_n.52.ids_ref
  104.9 49.6 %pick.2 = bf16[16,8,6144]{2,1,0:T(8,128)(2,1)} custom-call(s32[16]{0:T(128)} %select_n.52.ids_ref, bf16[16,8,6144]{2,1,0:T(8,128)(2,1)} %all-to-all-done.pool_ref), custom_call_target="tpu_custom_call" | custom-call | tf_op jit(solution)/shard_map/pick/pallas_call | solution.py:126
  154.4 0.0 all-to-all-done.2.pool_ref
  154.4 4.4 %all-to-all-start.1 = ((bf16[16,8,6144]{2,1,0:T(8,128)(2,1)}), bf16[16,8,6144]{2,1,0:T(8,128)(2,1)}, u32[]{:S(2)}, u32[]{:S(2)}) async-start(bf16[16,8,6144]{2,1,0:T(8,128)(2,1)} %pick.2), calls=%async_computation.1 | async-start | bytes 3145728 | tf_op jit(solution)/shard_map/all_to_all | solution.py:158
  158.9 33.7 %pick.3 = bf16[16,8,4096]{2,1,0:T(8,128)(2,1)} custom-call(s32[16]{0:T(128)} %select_n.52.ids_ref, bf16[16,8,4096]{2,1,0:T(8,128)(2,1)} %all-to-all-done.2.pool_ref), custom_call_target="tpu_custom_call" | custom-call | tf_op jit(solution)/shard_map/pick/pallas_call | solution.py:126
  192.6 0.0 all-to-all-done.1
  192.6 5.1 %all-to-all-start.3 = ((bf16[16,8,4096]{2,1,0:T(8,128)(2,1)}), bf16[16,8,4096]{2,1,0:T(8,128)(2,1)}, u32[]{:S(2)}, u32[]{:S(2)}) async-start(bf16[16,8,4096]{2,1,0:T(8,128)(2,1)} %pick.3), calls=%async_computation.3 | async-start | bytes 2097152 | tf_op jit(solution)/shard_map/all_to_all | solution.py:158
  199.0 0.0 copy-done
  199.0 3.0 %fusion.8.low_ref = bf16[256,128]{1,0:T(8,128)(2,1)} fusion(bf16[1,256,6144]{2,1,0:T(8,128)(2,1)S(1)} %copy-done, bf16[16,8,6144]{2,1,0:T(8,128)(2,1)} %all-to-all-done.1), kind=kOutput, calls=%fused_computation.5 | convolution fusion | flops 402685952 | bytes 4784128 | tf_op jit(solution)/shard_map/dot_general | solution.py:220
  202.0 11.9 %all-to-all-done.3 = bf16[16,8,4096]{2,1,0:T(8,128)(2,1)} async-done(((bf16[16,8,4096]{2,1,0:T(8,128)(2,1)}), bf16[16,8,4096]{2,1,0:T(8,128)(2,1)}, u32[]{:S(2)}, u32[]{:S(2)}) %all-to-all-start.3) | async-done | bytes 1048608 | tf_op jit(solution)/shard_map/all_to_all | solution.py:158
  213.8 18.2 %attention.1 = bf16[256,3072]{1,0:T(8,128)(2,1)} custom-call(s32[1]{0:T(128)S(6)} %copy.22.offset_ref, s32[1]{0:T(128)S(6)} %copy.21.length_ref, bf16[256,128]{1,0:T(8,128)(2,1)} %fusion.8.low_ref, bf16[128,4096]{1,0:T(8,128)(2,1)} %bitcast.11.up_q_ref.up_k_ref.up_v_ref, bf16[128,4096]{1,0:T(8,128)(2,1)} %bitcast.11.up_q_ref.up_k_ref.up_v_ref, ...), custom_call_target="tpu_custom_call" | custom-call | tf_op jit(solution)/shard_map/attention/pallas_call | solution.py:104
  (1 shorter events, 0.0 us)
Async XLA Ops:
  0.0 199.0 %copy-start = (bf16[1,256,6144]{2,1,0:T(8,128)(2,1)S(1)}, bf16[1,256,6144]{2,1,0:T(8,128)(2,1)}, u32[]{:S(2)}) copy-start(bf16[1,256,6144]{2,1,0:T(8,128)(2,1)} %param.11) | copy-start | bytes 9437188
  2.7 39.3 %all-to-all-start = ((bf16[16,8,6144]{2,1,0:T(8,128)(2,1)}), bf16[16,8,6144]{2,1,0:T(8,128)(2,1)}, u32[]{:S(2)}, u32[]{:S(2)}) async-start(bf16[16,8,6144]{2,1,0:T(8,128)(2,1)} %pad_maximum_fusion), calls=%async_computation | async-start | bytes 3145728 | tf_op jit(solution)/shard_map/all_to_all | solution.py:150
  11.2 40.0 %copy-start.1 = (s32[1,2]{1,0:T(1,128)S(1)}, s32[1,2]{1,0:T(1,128)}, u32[]{:S(2)}) copy-start(s32[1,2]{1,0:T(1,128)} %param.19) | copy-start | bytes 28
  42.0 112.4 %all-to-all-start.2 = ((bf16[16,8,4096]{2,1,0:T(8,128)(2,1)}), bf16[16,8,4096]{2,1,0:T(8,128)(2,1)}, u32[]{:S(2)}, u32[]{:S(2)}) async-start(bf16[16,8,4096]{2,1,0:T(8,128)(2,1)} %pad_maximum_fusion.1), calls=%async_computation.2 | async-start | bytes 2097152 | tf_op jit(solution)/shard_map/all_to_all | solution.py:150
  154.4 38.1 %all-to-all-start.1 = ((bf16[16,8,6144]{2,1,0:T(8,128)(2,1)}), bf16[16,8,6144]{2,1,0:T(8,128)(2,1)}, u32[]{:S(2)}, u32[]{:S(2)}) async-start(bf16[16,8,6144]{2,1,0:T(8,128)(2,1)} %pick.2), calls=%async_computation.1 | async-start | bytes 3145728 | tf_op jit(solution)/shard_map/all_to_all | solution.py:158
  192.6 21.3 %all-to-all-start.3 = ((bf16[16,8,4096]{2,1,0:T(8,128)(2,1)}), bf16[16,8,4096]{2,1,0:T(8,128)(2,1)}, u32[]{:S(2)}, u32[]{:S(2)}) async-start(bf16[16,8,4096]{2,1,0:T(8,128)(2,1)} %pick.3), calls=%async_computation.3 | async-start | bytes 2097152 | tf_op jit(solution)/shard_map/all_to_all | solution.py:158
where the time goes:
time: 233 us; the launch traced here: 232 us
  Pallas kernels  101 us (43%)
  blocking collectives  52.8 us (23%)
  waiting for transfers between devices  41.6 us (18%)
  starting transfers between devices  26.1 us (11%)
  other arithmetic  4.86 us (2%)
  matrix products  3 us (1%)
    pallas_call x2, Pallas kernels, pick(): pl.pallas_call(pick_kernel, grid_spec=pltpu.PrefetchScalarGridSpec(num_sc...  83.2 us
    all_gather x1, blocking collectives, body(): lax.all_gather(adapter_ids, ('groups', 'adapter'), axis=0, tiled=True)  52.8 us
    all_to_all x2, waiting for transfers between devices, spread(): return lax.all_to_all(doubled, 'adapter', 0, 0, tiled=True)  29.7 us
    pallas_call x1, Pallas kernels, attention(): pl.pallas_call(attention_kernel, grid_spec=grid_spec, out_shape=jax.Shape...  18.2 us
    all_to_all x2, starting transfers between devices, spread(): return lax.all_to_all(doubled, 'adapter', 0, 0, tiled=True)  16.6 us
    all_to_all x2, waiting for transfers between devices, gather(): lax.all_to_all(picked, ('groups', 'adapter'), 0, 0, tiled=True, axis_inde...  11.9 us
    all_to_all x2, starting transfers between devices, gather(): lax.all_to_all(picked, ('groups', 'adapter'), 0, 0, tiled=True, axis_inde...  9.5 us
  transfers between devices with their start and end apart: 4, of which 2 were waited for; matrix products, arithmetic and copies ran while one was open for 3% of the time, Pallas kernels for 36%

commit v1 on v0

--- a/solution.py
+++ b/solution.py
@@ -14,6 +14,7 @@
 STRETCH = 256
 CACHE = 1024
 ROWS = 8
+LANES = 128
 
 
 def attention_kernel(
@@ -110,19 +111,29 @@
     )(offset, length, low, up, up, up, base, base, base, cache_keys, cache_values)
 
 
-def pick_kernel(ids_ref, pool_ref, out_ref, sem):
-    copies = [
-        pltpu.make_async_copy(pool_ref.at[ids_ref[i]], out_ref.at[i], sem.at[i])
-        for i in range(out_ref.shape[0])
+def pick_kernel(ids_ref, pool_ref, out_ref, held, in_sem, out_sem):
+    count, _, width = out_ref.shape
+    reads = [
+        pltpu.make_async_copy(
+            pool_ref.at[ids_ref[i], :, pl.ds(0, width)], held.at[i], in_sem.at[i]
+        )
+        for i in range(count)
     ]
-    for copy in copies:
-        copy.start()
-    for copy in copies:
-        copy.wait()
-
-
-def pick(pool, ids):
+    writes = [
+        pltpu.make_async_copy(held.at[i], out_ref.at[i], out_sem.at[i]) for i in range(count)
+    ]
+    for read in reads:
+        read.start()
+    for read, write in zip(reads, writes):
+        read.wait()
+        write.start()
+    for write in writes:
+        write.wait()
+
+
+def pick(pool, ids, width):
     count = ids.shape[0]
+    rows = pool.shape[1]
     return pl.pallas_call(
         pick_kernel,
         grid_spec=pltpu.PrefetchScalarGridSpec(
@@ -130,43 +141,63 @@
             grid=(1,),
             in_specs=[pl.BlockSpec(memory_space=pl.ANY)],
             out_specs=pl.BlockSpec(memory_space=pl.ANY),
-            scratch_shapes=[pltpu.SemaphoreType.DMA((count,))],
+            scratch_shapes=[
+                pltpu.VMEM((count, rows, width), pool.dtype),
+                pltpu.SemaphoreType.DMA((count,)),
+                pltpu.SemaphoreType.DMA((count,)),
+            ],
         ),
-        out_shape=jax.ShapeDtypeStruct((count,) + pool.shape[1:], pool.dtype),
+        out_shape=jax.ShapeDtypeStruct((count, rows, width), pool.dtype),
         name="pick",
     )(ids, pool)
 
 
-def fetch_halves(down, up, ids_all):
+def fetch_halves(down, up, ids):
     group = lax.axis_index("groups")
     index = lax.axis_index("adapter")
-    half = index // 8
-    rank = down.shape[1]
-
-    def spread(pair):
-        mine = jnp.where(group == 0, pair[0], pair[1])
-        blocks = mine.reshape(rank // ROWS, ROWS, mine.shape[-1])
-        doubled = jnp.concatenate([blocks, blocks], axis=0)
+    rank, down_width = down[0].shape
+    up_width = up[0].shape[1]
+    blocks = rank // ROWS
+
+    other_ids = lax.ppermute(ids, "groups", [(0, 1), (1, 0)])
+    both_ids = jnp.where(group == 0, jnp.stack([ids, other_ids]), jnp.stack([other_ids, ids]))
+    note = jnp.pad(
+        both_ids.reshape(1, 1, 4).astype(jnp.bfloat16), ((0, 0), (0, ROWS - 1), (0, LANES - 4))
+    )
+    note = jnp.broadcast_to(note, (blocks, ROWS, LANES))
+
+    def spread(pair, extra=None):
+        mine = jnp.where(group == 0, pair[0], pair[1]).reshape(blocks, ROWS, -1)
+        if extra is not None:
+            mine = jnp.concatenate([mine, extra], axis=-1)
+        doubled = jnp.concatenate([mine, mine], axis=0)
         return lax.all_to_all(doubled, "adapter", 0, 0, tiled=True)
 
     members = [[g * 16 + h * 8 + k for g in range(2) for k in range(8)] for h in range(2)]
-    wanted = lax.dynamic_slice_in_dim(ids_all, half * 8, 8, axis=1)
-    wanted = jnp.where(group == 0, wanted[..., 0], wanted[..., 1]).reshape(16)
-
-    def gather(pool):
-        picked = pick(pool, wanted)
+
+    down_pool = spread(down, note)
+    up_pool = spread(up)
+    notes = down_pool[:, 0, down_width : down_width + 4].astype(jnp.int32)
+    lower = index < 8
+    notes = jnp.where(lower, notes[:8], notes[8:]).reshape(8, 2, 2)
+    wanted = jnp.where(group == 0, notes[..., 0], notes[..., 1]).T.reshape(16)
+
+    def gather(pool, width):
+        picked = pick(pool, wanted, width)
         got = lax.all_to_all(
             picked, ("groups", "adapter"), 0, 0, tiled=True, axis_index_groups=members
         )
-        return got.reshape(2 * rank, pool.shape[-1])
-
-    down_pool = spread(down)
-    up_pool = spread(up)
-    return gather(down_pool), gather(up_pool)
-
-
-def fetch_any(down, up, ids_all):
-    adapters = ids_all.shape[1]
+        return got.reshape(2 * rank, width)
+
+    return gather(down_pool, down_width), gather(up_pool, up_width)
+
+
+def fetch_any(down, up, ids):
+    adapters = lax.axis_size("adapter")
+    ids_all = lax.all_gather(ids, ("groups", "adapter"), axis=0, tiled=True)
+    ids_all = ids_all.reshape(-1, adapters, 2)
+    down = jnp.stack(down)
+    up = jnp.stack(up)
     group = lax.axis_index("groups")
     rank = down.shape[1]
     parts = adapters // (rank // ROWS)
@@ -203,20 +234,10 @@
     offsets,
     halves,
 ):
-    ids_all = lax.all_gather(adapter_ids, ("groups", "adapter"), axis=0, tiled=True)
-    ids_all = ids_all.reshape(2, -1, 2)
     down = (persona_down[0].T, domain_down[0].T)
     up = (persona_up[0].T, domain_up[0].T)
-    if halves:
-        fetch = fetch_halves
-    else:
-        fetch = fetch_any
-        down = jnp.stack(down)
-        up = jnp.stack(up)
-    if halves:
-        down_mine, up_mine = fetch(_Pair(down), _Pair(up), ids_all)
-    else:
-        down_mine, up_mine = fetch(down, up, ids_all)
+    fetch = fetch_halves if halves else fetch_any
+    down_mine, up_mine = fetch(down, up, adapter_ids)
     low = lax.dot_general(
         tokens[0],
         down_mine,
@@ -227,15 +248,6 @@
     return out[None]
 
 
-class _Pair:
-    def __init__(self, items):
-        self.items = items
-        self.shape = (2,) + items[0].shape
-
-    def __getitem__(self, at):
-        return self.items[at]
-
-
 def solution(mesh):
     both = ("groups", "adapter")
     in_specs = (

time: 233 us -> 148 us (0.64)
  Pallas kernels: 101 us -> 24.7 us
  blocking collectives: 52.8 us -> 0 us
  waiting for transfers between devices: 41.6 us -> 79.5 us
  starting transfers between devices: 26.1 us -> 29.6 us
  other arithmetic: 4.86 us -> 7.75 us
    pallas_call x2, Pallas kernels: 83.2 us -> 6.54 us  [pick(): pl.pallas_call(pick_kernel, grid_spec=pltpu.PrefetchScalarGridSpec(num_sc...]
    all_gather x1 -> x0, blocking collectives: 52.8 us -> none  [body(): lax.all_gather(adapter_ids, ('groups', 'adapter'), axis=0, tiled=True)]
    all_to_all x2, waiting for transfers between devices: 11.9 us -> 31.3 us  [gather(): lax.all_to_all(picked, ('groups', 'adapter'), 0, 0, tiled=True, axis_inde...]
    all_to_all x2, waiting for transfers between devices: 29.7 us -> 48.2 us  [spread(): return lax.all_to_all(doubled, 'adapter', 0, 0, tiled=True)]
    ppermute x0 -> x1, starting transfers between devices: none -> 3 us  [fetch_halves(): other_ids = lax.ppermute(ids, 'groups', [(0, 1), (1, 0)])]
  transfers between devices with their start and end apart: 4 -> 5, of which waited for: 2 -> 4; matrix products, arithmetic and copies ran while one was open for 3% -> 6% of each run, Pallas kernels for 36% -> 4%
where the time goes in v1:
time: 148 us; the launch traced here: 147 us
  waiting for transfers between devices  79.5 us (54%)
  starting transfers between devices  29.6 us (20%)
  Pallas kernels  24.7 us (17%)
  other arithmetic  7.75 us (5%)
  matrix products  3 us (2%)
    all_to_all x2, waiting for transfers between devices, spread(): return lax.all_to_all(doubled, 'adapter', 0, 0, tiled=True)  48.2 us
    all_to_all x2, waiting for transfers between devices, gather(): lax.all_to_all(picked, ('groups', 'adapter'), 0, 0, tiled=True, axis_inde...  31.3 us
    pallas_call x1, Pallas kernels, attention(): pl.pallas_call(attention_kernel, grid_spec=grid_spec, out_shape=jax.Shape...  18.2 us
    all_to_all x2, starting transfers between devices, spread(): return lax.all_to_all(doubled, 'adapter', 0, 0, tiled=True)  15.3 us
    all_to_all x2, starting transfers between devices, gather(): lax.all_to_all(picked, ('groups', 'adapter'), 0, 0, tiled=True, axis_inde...  11.2 us
    pallas_call x2, Pallas kernels, pick(): pl.pallas_call(pick_kernel, grid_spec=pltpu.PrefetchScalarGridSpec(num_sc...  6.54 us
    concatenate x2, other arithmetic, spread(): doubled = jnp.concatenate([mine, mine], axis=0)  3.73 us
    reshape x2, other arithmetic, spread(): mine = jnp.where(group == 0, pair[0], pair[1]).reshape(blocks, ROWS, -1)  3.21 us
  transfers between devices with their start and end apart: 5, of which 4 were waited for; matrix products, arithmetic and copies ran while one was open for 6% of the time, Pallas kernels for 4%

profile of v1, /device:TPU:0, one launch (start us, length us, event | category | flops | bytes accessed | tf_op | source)
XLA Modules:
  0.0 146.8 jit_solution(3341249961022688347)
XLA Ops:
  0.0 0.0 copy-start
  0.0 0.0 copy-start.1
  0.0 3.0 %collective-permute-start = (s32[1,2]{1,0:T(1,128)}, s32[1,2]{1,0:T(1,128)S(1)}, u32[]{:S(2)}, u32[]{:S(2)}) collective-permute-start(s32[1,2]{1,0:T(1,128)} %param.19), channel_id=1, source_target_pairs={{0,16},{16,0},{1,17},{17,1},{2,18},{18,2},{3,19},{19,3},{4,20},{20... | collective-permute-start | bytes 32 | tf_op jit(solution)/shard_map/ppermute | solution.py:162
  3.0 2.1 %select_bitcast_fusion = bf16[8,8,6144]{2,1,0:T(8,128)(2,1)} fusion(bf16[1,6144,64]{1,2,0:T(8,128)(2,1)} %param.15, bf16[1,6144,64]{1,2,0:T(8,128)(2,1)} %param.16, pred[]{:T(512)S(6)} %eq.2), kind=kLoop, calls=%fused_computation.7 | loop fusion | flops 393216 | bytes 2359297 | tf_op jit(solution)/shard_map/reshape | solution.py:170
  5.1 0.0 collective-permute-done
  5.1 0.0 copy-done.1
  5.1 0.1 convert_element_type.26
  5.2 2.6 %maximum_maximum_fusion = bf16[16,8,6272]{2,1,0:T(8,128)(2,1)} fusion(bf16[8,8,128]{2,1,0:T(8,128)(2,1)S(1)} %broadcast_in_dim.11, bf16[8,8,6144]{2,1,0:T(8,128)(2,1)} %select_bitcast_fusion), kind=kLoop, calls=%fused_computation.2 | loop fusion | flops 6422528 | bytes 2408448 | tf_op jit(solution)/shard_map/concatenate | solution.py:173
  7.9 6.0 %all-to-all-start = ((bf16[16,8,6272]{2,1,0:T(8,128)(2,1)}), bf16[16,8,6272]{2,1,0:T(8,128)(2,1)}, u32[]{:S(2)}, u32[]{:S(2)}) async-start(bf16[16,8,6272]{2,1,0:T(8,128)(2,1)} %maximum_maximum_fusion), calls=%async_computation | async-start | bytes 3211264 | tf_op jit(solution)/shard_map/all_to_all | solution.py:174
  13.9 1.1 select_bitcast_fusion.1
  15.0 1.1 pad_maximum_fusion
  16.1 30.3 %all-to-all-done.pool_ref = bf16[16,8,6272]{2,1,0:T(8,128)(2,1)} async-done(((bf16[16,8,6272]{2,1,0:T(8,128)(2,1)}), bf16[16,8,6272]{2,1,0:T(8,128)(2,1)}, u32[]{:S(2)}, u32[]{:S(2)}) %all-to-all-start) | async-done | bytes 1605664 | tf_op jit(solution)/shard_map/all_to_all | solution.py:174
  46.4 9.3 %all-to-all-start.2 = ((bf16[16,8,4096]{2,1,0:T(8,128)(2,1)}), bf16[16,8,4096]{2,1,0:T(8,128)(2,1)}, u32[]{:S(2)}, u32[]{:S(2)}) async-start(bf16[16,8,4096]{2,1,0:T(8,128)(2,1)} %pad_maximum_fusion), calls=%async_computation.2 | async-start | bytes 2097152 | tf_op jit(solution)/shard_map/all_to_all | solution.py:174
  55.7 0.8 slice_convert_fusion
  56.5 0.1 copy.14
  56.6 0.7 reshape.77.ids_ref
  57.3 3.5 %pick.2 = bf16[16,8,6144]{2,1,0:T(8,128)(2,1)} custom-call(s32[16]{0:T(128)} %reshape.77.ids_ref, bf16[16,8,6272]{2,1,0:T(8,128)(2,1)} %all-to-all-done.pool_ref), custom_call_target="tpu_custom_call" | custom-call | tf_op jit(solution)/shard_map/pick/pallas_call | solution.py:137
  60.7 17.9 %all-to-all-done.2.pool_ref = bf16[16,8,4096]{2,1,0:T(8,128)(2,1)} async-done(((bf16[16,8,4096]{2,1,0:T(8,128)(2,1)}), bf16[16,8,4096]{2,1,0:T(8,128)(2,1)}, u32[]{:S(2)}, u32[]{:S(2)}) %all-to-all-start.2) | async-done | bytes 1048608 | tf_op jit(solution)/shard_map/all_to_all | solution.py:174
  78.6 6.9 %all-to-all-start.1 = ((bf16[16,8,6144]{2,1,0:T(8,128)(2,1)}), bf16[16,8,6144]{2,1,0:T(8,128)(2,1)}, u32[]{:S(2)}, u32[]{:S(2)}) async-start(bf16[16,8,6144]{2,1,0:T(8,128)(2,1)} %pick.2), calls=%async_computation.1 | async-start | bytes 3145728 | tf_op jit(solution)/shard_map/all_to_all | solution.py:187
  85.5 3.1 %pick.3 = bf16[16,8,4096]{2,1,0:T(8,128)(2,1)} custom-call(s32[16]{0:T(128)} %reshape.77.ids_ref, bf16[16,8,4096]{2,1,0:T(8,128)(2,1)} %all-to-all-done.2.pool_ref), custom_call_target="tpu_custom_call" | custom-call | tf_op jit(solution)/shard_map/pick/pallas_call | solution.py:137
  88.6 19.5 %all-to-all-done.1 = bf16[16,8,6144]{2,1,0:T(8,128)(2,1)} async-done(((bf16[16,8,6144]{2,1,0:T(8,128)(2,1)}), bf16[16,8,6144]{2,1,0:T(8,128)(2,1)}, u32[]{:S(2)}, u32[]{:S(2)}) %all-to-all-start.1) | async-done | bytes 1572896 | tf_op jit(solution)/shard_map/all_to_all | solution.py:187
  108.1 4.3 %all-to-all-start.3 = ((bf16[16,8,4096]{2,1,0:T(8,128)(2,1)}), bf16[16,8,4096]{2,1,0:T(8,128)(2,1)}, u32[]{:S(2)}, u32[]{:S(2)}) async-start(bf16[16,8,4096]{2,1,0:T(8,128)(2,1)} %pick.3), calls=%async_computation.3 | async-start | bytes 2097152 | tf_op jit(solution)/shard_map/all_to_all | solution.py:187
  113.7 0.0 copy-done
  113.8 3.0 %fusion.8.low_ref = bf16[256,128]{1,0:T(8,128)(2,1)} fusion(bf16[1,256,6144]{2,1,0:T(8,128)(2,1)S(1)} %copy-done, bf16[16,8,6144]{2,1,0:T(8,128)(2,1)} %all-to-all-done.1), kind=kOutput, calls=%fused_computation.5 | convolution fusion | flops 402685952 | bytes 4784128 | tf_op jit(solution)/shard_map/dot_general | solution.py:241
  116.8 11.8 %all-to-all-done.3 = bf16[16,8,4096]{2,1,0:T(8,128)(2,1)} async-done(((bf16[16,8,4096]{2,1,0:T(8,128)(2,1)}), bf16[16,8,4096]{2,1,0:T(8,128)(2,1)}, u32[]{:S(2)}, u32[]{:S(2)}) %all-to-all-start.3) | async-done | bytes 1048608 | tf_op jit(solution)/shard_map/all_to_all | solution.py:187
  128.6 18.2 %attention.1 = bf16[256,3072]{1,0:T(8,128)(2,1)} custom-call(s32[1]{0:T(128)S(6)} %copy.18.offset_ref, s32[1]{0:T(128)S(6)} %copy.17.length_ref, bf16[256,128]{1,0:T(8,128)(2,1)} %fusion.8.low_ref, bf16[128,4096]{1,0:T(8,128)(2,1)} %bitcast.15.up_q_ref.up_k_ref.up_v_ref, bf16[128,4096]{1,0:T(8,128)(2,1)} %bitcast.15.up_q_ref.up_k_ref.up_v_ref, ...), custom_call_target="tpu_custom_call" | custom-call | tf_op jit(solution)/shard_map/attention/pallas_call | solution.py:105
  (5 shorter events, 0.1 us)
Async XLA Ops:
  0.0 113.8 %copy-start = (bf16[1,256,6144]{2,1,0:T(8,128)(2,1)S(1)}, bf16[1,256,6144]{2,1,0:T(8,128)(2,1)}, u32[]{:S(2)}) copy-start(bf16[1,256,6144]{2,1,0:T(8,128)(2,1)} %param.11) | copy-start | bytes 9437188
  0.0 5.1 %copy-start.1 = (s32[1,2]{1,0:T(1,128)S(1)}, s32[1,2]{1,0:T(1,128)}, u32[]{:S(2)}) copy-start(s32[1,2]{1,0:T(1,128)} %param.19) | copy-start | bytes 28
  0.0 5.1 %collective-permute-start = (s32[1,2]{1,0:T(1,128)}, s32[1,2]{1,0:T(1,128)S(1)}, u32[]{:S(2)}, u32[]{:S(2)}) collective-permute-start(s32[1,2]{1,0:T(1,128)} %param.19), channel_id=1, source_target_pairs={{0,16},{16,0},{1,17},{17,1},{2,18},{18,2},{3,19},{19,3},{4,20},{20... | collective-permute-start | bytes 32 | tf_op jit(solution)/shard_map/ppermute | solution.py:162
  7.9 38.5 %all-to-all-start = ((bf16[16,8,6272]{2,1,0:T(8,128)(2,1)}), bf16[16,8,6272]{2,1,0:T(8,128)(2,1)}, u32[]{:S(2)}, u32[]{:S(2)}) async-start(bf16[16,8,6272]{2,1,0:T(8,128)(2,1)} %maximum_maximum_fusion), calls=%async_computation | async-start | bytes 3211264 | tf_op jit(solution)/shard_map/all_to_all | solution.py:174
  46.4 32.2 %all-to-all-start.2 = ((bf16[16,8,4096]{2,1,0:T(8,128)(2,1)}), bf16[16,8,4096]{2,1,0:T(8,128)(2,1)}, u32[]{:S(2)}, u32[]{:S(2)}) async-start(bf16[16,8,4096]{2,1,0:T(8,128)(2,1)} %pad_maximum_fusion), calls=%async_computation.2 | async-start | bytes 2097152 | tf_op jit(solution)/shard_map/all_to_all | solution.py:174
  78.6 29.5 %all-to-all-start.1 = ((bf16[16,8,6144]{2,1,0:T(8,128)(2,1)}), bf16[16,8,6144]{2,1,0:T(8,128)(2,1)}, u32[]{:S(2)}, u32[]{:S(2)}) async-start(bf16[16,8,6144]{2,1,0:T(8,128)(2,1)} %pick.2), calls=%async_computation.1 | async-start | bytes 3145728 | tf_op jit(solution)/shard_map/all_to_all | solution.py:187
  108.1 20.5 %all-to-all-start.3 = ((bf16[16,8,4096]{2,1,0:T(8,128)(2,1)}), bf16[16,8,4096]{2,1,0:T(8,128)(2,1)}, u32[]{:S(2)}, u32[]{:S(2)}) async-start(bf16[16,8,4096]{2,1,0:T(8,128)(2,1)} %pick.3), calls=%async_computation.3 | async-start | bytes 2097152 | tf_op jit(solution)/shard_map/all_to_all | solution.py:187
